TPU v7x, 32 devices: a whole 2x2x4 slice. The times are simulated.
32 devices in a mesh: groups: 2 (over y), blk: 4 (over z), tile: 2 (over x), pair: 2 (over core).
Axes of the slice: x: 2, y: 2, z: 4, core: 2. Of those that a mesh axis runs over, the one named last changes fastest.
Arguments:
- left_tokens: bfloat16 [4, 1536, 768], P(('groups', 'pair'), 'blk', 'tile'), parts along dimension 0, may hold values from -32 to 32
- right_tokens: bfloat16 [4, 1536, 768], P(('groups', 'pair'), 'blk', 'tile'), parts along dimension 0, may hold values from -32 to 32
- self_qkv: bfloat16 [3, 768, 512], P(None, None, 'tile'), may hold values from -1 to 1
- self_out: bfloat16 [512, 768], P('tile'), may hold values from -0.25 to 0.25
- cross_qkv: bfloat16 [3, 768, 512], P(None, None, 'tile'), may hold values from -1 to 1
- cross_out: bfloat16 [512, 768], P('tile'), may hold values from -0.25 to 0.25
- reassemble: bfloat16 [768, 256], P('tile'), may hold values from -0.21875 to 0.21875
- conv_weight: bfloat16 [3, 3, 256, 256], replicated, may hold values from -0.125 to 0.125
Outputs:
- joined: bfloat16 [4, 12, 128, 256], P(('groups', 'pair'), 'blk', 'tile'), parts along dimension 0
There are 2 independent parts, one for each index of `groups`. A program takes and returns all parts, laid end to end along the dimension named above; an argument that names none is the same for every part. Nothing has to cross between parts.
All inputs are finite; a program needn't handle non-finite values.
Results may differ from a plain program's by a relative error of at most 0.018.
Values may be sent and summed in bfloat16 or wider, within the bound.
A program may use at most 64 MiB of HBM per device.

v0:
```python
import jax
import jax.numpy as jnp
from jax import lax
from jax.sharding import PartitionSpec as P

HD = 64
CH = 256
GRID_W = 128


def padded_2(cells, sides, width):
    for axis, dim in sides:
        count = lax.axis_size(axis)
        ends = count - 1
        head = lax.slice_in_dim(cells, 0, width, axis=dim)
        tail = lax.slice_in_dim(cells, cells.shape[dim] - width, cells.shape[dim], axis=dim)
        cells = jnp.concatenate(
            [
                lax.ppermute(tail, axis, [(i, (i + 1) % count) for i in range(ends)]),
                cells,
                lax.ppermute(head, axis, [((i + 1) % count, i) for i in range(ends)]),
            ],
            axis=dim,
        )
    return cells


def layer_norm(values):
    widened = values.astype(jnp.float32)
    centred = widened - jnp.mean(widened, axis=-1, keepdims=True)
    variance = jnp.mean(centred * centred, axis=-1, keepdims=True)
    return (centred * lax.rsqrt(variance + 1e-06)).astype(jnp.bfloat16)


def project_rows(normed, weight):
    return jnp.dot(normed, weight, preferred_element_type=jnp.float32).astype(jnp.bfloat16)


def initial_state(queries):
    query_count = queries.shape[0]
    head_count = queries.shape[1] // HD
    return (
        jnp.full((head_count, query_count), -1e30, jnp.float32),
        jnp.zeros((head_count, query_count), jnp.float32),
        jnp.zeros(queries.shape, jnp.float32),
    )


def attend_keys(running, queries, keys_rows, values_rows):
    maxima, totals, accumulated = running
    query_count = queries.shape[0]
    head_count = queries.shape[1] // HD
    key_count = keys_rows.shape[0]
    scores = jnp.einsum(
        "qhd,khd->hqk",
        queries.reshape(query_count, head_count, HD),
        keys_rows.reshape(key_count, head_count, HD),
        preferred_element_type=jnp.float32,
    ) * HD ** (-0.5)
    new_maxima = jnp.maximum(maxima, jnp.max(scores, axis=2))
    correction = jnp.exp(maxima - new_maxima)
    expanded = jnp.exp(scores - new_maxima[:, :, None])
    totals = totals * correction + jnp.sum(expanded, axis=2)
    mixed = jnp.einsum(
        "hqk,khd->qhd",
        expanded.astype(jnp.bfloat16),
        values_rows.reshape(key_count, head_count, HD),
        preferred_element_type=jnp.float32,
    )
    accumulated = (
        accumulated.reshape(query_count, head_count, HD) * correction.T[:, :, None] + mixed
    )
    return (new_maxima, totals, accumulated.reshape(query_count, head_count * HD))


def fold_keys(running, queries, keys_rows, values_rows):
    key_count = keys_rows.shape[0]
    block_rows = max((divisor for divisor in range(1, 1025) if key_count % divisor == 0))
    if block_rows == key_count:
        return attend_keys(running, queries, keys_rows, values_rows)
    stacked_keys = keys_rows.reshape(key_count // block_rows, block_rows, keys_rows.shape[1])
    stacked_values = values_rows.reshape(key_count // block_rows, block_rows, values_rows.shape[1])

    def step_block(current, blocks):
        return (attend_keys(current, queries, blocks[0], blocks[1]), None)

    result, unused = lax.scan(step_block, running, (stacked_keys, stacked_values))
    return result


def finish_state(running):
    maxima, totals, accumulated = running
    query_count = accumulated.shape[0]
    head_count = accumulated.shape[1] // HD
    normalized = accumulated.reshape(query_count, head_count, HD) / totals.T[:, :, None]
    return normalized.reshape(query_count, head_count * HD).astype(jnp.bfloat16)


def body(
    left_tokens, right_tokens, self_qkv, self_out, cross_qkv, cross_out, reassemble, conv_weight
):
    left_full, right_full = (
        lax.all_gather(left_tokens, "tile", axis=2, tiled=True),
        lax.all_gather(right_tokens, "tile", axis=2, tiled=True),
    )
    left_rows = left_full[0]
    left_normed = layer_norm(left_rows)
    right_normed = layer_norm(right_full[0])
    self_query = project_rows(left_normed, self_qkv[0])
    self_key = project_rows(left_normed, self_qkv[1])
    self_value = project_rows(left_normed, self_qkv[2])
    cross_key = project_rows(right_normed, cross_qkv[1])
    cross_value = project_rows(right_normed, cross_qkv[2])
    pieces = (
        lax.all_gather(self_key, "blk", axis=0, tiled=True),
        lax.all_gather(self_value, "blk", axis=0, tiled=True),
    )
    self_state = fold_keys(initial_state(self_query), self_query, pieces[0], pieces[1])
    self_mixed = finish_state(self_state)
    self_term = jnp.dot(self_mixed, self_out, preferred_element_type=jnp.float32)
    self_share = lax.psum_scatter(
        self_term.astype(jnp.bfloat16), "tile", scatter_dimension=1, tiled=True
    ).astype(jnp.float32)
    updated = (left_tokens[0].astype(jnp.float32) + self_share).astype(jnp.bfloat16)
    updated_full = lax.all_gather(updated, "tile", axis=1, tiled=True)
    updated_normed = layer_norm(updated_full)
    cross_query = project_rows(updated_normed, cross_qkv[0])
    pieces = (
        lax.all_gather(cross_key, "blk", axis=0, tiled=True),
        lax.all_gather(cross_value, "blk", axis=0, tiled=True),
    )
    cross_state = fold_keys(initial_state(cross_query), cross_query, pieces[0], pieces[1])
    cross_mixed = finish_state(cross_state)
    cross_share = lax.psum_scatter(
        jnp.dot(cross_mixed, cross_out, preferred_element_type=jnp.float32).astype(jnp.bfloat16),
        "tile",
        scatter_dimension=1,
        tiled=True,
    ).astype(jnp.float32)
    final_tokens = (updated.astype(jnp.float32) + cross_share).astype(jnp.bfloat16)
    band_rows = final_tokens.shape[0] // GRID_W
    partial_map = jnp.dot(final_tokens, reassemble, preferred_element_type=jnp.float32).reshape(
        band_rows, GRID_W, CH
    )
    feature_map = lax.psum_scatter(
        partial_map.astype(jnp.bfloat16), "tile", scatter_dimension=1, tiled=True
    )
    column_count = feature_map.shape[1]
    activated = jnp.maximum(feature_map, jnp.zeros((), jnp.bfloat16))
    padded = padded_2(activated, (("blk", 0), ("tile", 1)), 1)
    stacked = jnp.concatenate(
        [
            padded[row_shift : row_shift + band_rows, col_shift : col_shift + column_count]
            for row_shift in range(3)
            for col_shift in range(3)
        ],
        axis=-1,
    )
    convolved = jnp.dot(
        stacked.reshape(band_rows * column_count, 9 * CH),
        conv_weight.reshape(9 * CH, CH),
        preferred_element_type=jnp.float32,
    )
    joined = (
        feature_map.astype(jnp.float32) + convolved.reshape(band_rows, column_count, CH)
    ).astype(jnp.bfloat16)
    return joined[None]


def solution(mesh):
    placed = (
        P(("groups", "pair"), "blk", "tile"),
        P(("groups", "pair"), "blk", "tile"),
        P(None, None, "tile"),
        P("tile", None),
        P(None, None, "tile"),
        P("tile", None),
        P("tile", None),
        P(),
    )
    return jax.shard_map(
        body,
        mesh=mesh,
        in_specs=placed,
        out_specs=P(("groups", "pair"), "blk", "tile", None),
        check_vma=False,
    )
```

profile of v0, /device:TPU:0, one launch (start us, length us, event | category | flops | bytes accessed | tf_op | source)
XLA Modules:
  0.0 217.8 jit_solution(9744858873867985740)
XLA Ops:
  6.5 11.0 %all_gather.21 = bf16[1,384,768]{2,1,0:T(8,128)(2,1)S(1)} all-gather(bf16[1,384,384]{2,1,0:T(8,128)(2,1)} %param.12), channel_id=1, replica_groups=mesh['groups'=2,'blk'=4,'tile'=2,'pair'=2] {'tile'}, dimensions={2}, use_global_device_ids=true | all-gather | bytes 884736 | tf_op jit(solution)/shard_map/all_gather | solution.py:103
  18.1 1.4 convolution_convert_fusion.8
  20.3 20.0 %all_gather.22 = bf16[1536,256]{1,0:T(8,128)(2,1)S(1)} all-gather(bf16[384,256]{1,0:T(8,128)(2,1)S(1)} %convolution_convert_fusion.8), channel_id=1, replica_groups=mesh['groups'=2,'blk'=4,'tile'=2,'pair'=2] {'blk'}, dimensions={0}, use_global_device_ids=true | all-gather | bytes 983040 | tf_op jit(solution)/shard_map/all_gather | solution.py:115
  40.3 18.1 %all_gather.23 = bf16[1536,256]{1,0:T(8,128)(2,1)} all-gather(bf16[384,256]{1,0:T(8,128)(2,1)S(1)} %convolution_convert_fusion.6), channel_id=1, replica_groups=mesh['groups'=2,'blk'=4,'tile'=2,'pair'=2] {'blk'}, dimensions={0}, use_global_device_ids=true | all-gather | bytes 983040 | tf_op jit(solution)/shard_map/all_gather | solution.py:116
  58.4 0.8 copy.20
  59.3 19.8 %while.30 = (s32[]{:T(128)}, f32[4,384]{1,0:T(4,128)S(1)}, f32[4,384]{1,0:T(4,128)S(1)}, f32[384,256]{0,1:T(8,128)S(1)}, bf16[2,768,256]{2,1,0:T(8,128)(2,1)S(1)...) while((s32[]{:T(128)}, f32[4,384]{1,0:T(4,128)S(1)}, ...), condition=%wide.region_5.0_spmd.clone, body=%wide.region_2.5_spmd.clone.sunk | while | flops 311632896 | bytes 38043784 | solution.py:87
  59.3 1.1 constant_dynamic-slice_fusion.6
  60.5 3.9 %bitcast_reduce_fusion.4 = (f32[4,384]{1,0:T(4,128)S(1)}, f32[4,768,384]{2,1,0:T(8,128)}) fusion(bf16[768,4,64]{0,2,1:T(8,128)(2,1)S(1)} %bitcast.186, bf16[384,4,64]{0,2,1:T(8,128)(2,1)} %bitcast.199), kind=kOutput, calls=%fused_computation.1.clone.1 | convolution fusion | flops 153352704 | bytes 5314560 | tf_op jit(solution)/shard_map/while/body/eval_jaxpr/qhd,khd->hqk/dot_general | solution.py:54
  64.6 3.5 %fusion.112 = f32[384,4,64]{0,2,1:T(8,128)S(1)} fusion(bf16[768,4,64]{0,2,1:T(8,128)(2,1)S(1)} %bitcast.187, f32[4,768,384]{2,1,0:T(8,128)} %get-tuple-element.301, f32[4,384]{1,0:T(4,128)S(1)} %get-tuple-element.336, f32[384,4,64]{0,2,1:T(8,128)S(1)} %bitcast.192, f32[384,4]{0,1:T(4,128)S(1)} %get-tuple-element.303), kind=kOutput, calls=%fused_computation.9.clone.1 | convolution fusion | flops 154730496 | bytes 5910528 | tf_op jit(solution)/shard_map/while/body/eval_jaxpr/hqk,khd->qhd/dot_general | solution.py:64
  68.3 0.8 fusion.110
  69.2 1.1 constant_dynamic-slice_fusion.6
  70.4 3.9 %bitcast_reduce_fusion.4 = (f32[4,384]{1,0:T(4,128)S(1)}, f32[4,768,384]{2,1,0:T(8,128)}) fusion(bf16[768,4,64]{0,2,1:T(8,128)(2,1)S(1)} %bitcast.186, bf16[384,4,64]{0,2,1:T(8,128)(2,1)} %bitcast.199), kind=kOutput, calls=%fused_computation.1.clone.1 | convolution fusion | flops 153352704 | bytes 5314560 | tf_op jit(solution)/shard_map/while/body/eval_jaxpr/qhd,khd->hqk/dot_general | solution.py:54
  74.5 3.5 %fusion.112 = f32[384,4,64]{0,2,1:T(8,128)S(1)} fusion(bf16[768,4,64]{0,2,1:T(8,128)(2,1)S(1)} %bitcast.187, f32[4,768,384]{2,1,0:T(8,128)} %get-tuple-element.301, f32[4,384]{1,0:T(4,128)S(1)} %get-tuple-element.336, f32[384,4,64]{0,2,1:T(8,128)S(1)} %bitcast.192, f32[384,4]{0,1:T(4,128)S(1)} %get-tuple-element.303), kind=kOutput, calls=%fused_computation.9.clone.1 | convolution fusion | flops 154730496 | bytes 5910528 | tf_op jit(solution)/shard_map/while/body/eval_jaxpr/hqk,khd->qhd/dot_general | solution.py:64
  78.2 0.8 fusion.110
  79.1 1.4 convolution_convert_fusion.1
  80.5 1.0 copy.27
  81.6 9.7 %all_gather.24 = bf16[1,384,768]{2,1,0:T(8,128)(2,1)S(1)} all-gather(bf16[1,384,384]{2,1,0:T(8,128)(2,1)S(1)} %copy-done.7), channel_id=1, replica_groups=mesh['groups'=2,'blk'=4,'tile'=2,'pair'=2] {'tile'}, dimensions={2}, use_global_device_ids=true | all-gather | bytes 884736 | tf_op jit(solution)/shard_map/all_gather | solution.py:104
  91.8 1.4 convolution_convert_fusion.3
  93.2 1.4 convolution_convert_fusion.5
  94.6 17.3 %all_gather.27 = bf16[1536,256]{1,0:T(8,128)(2,1)S(1)} all-gather(bf16[384,256]{1,0:T(8,128)(2,1)S(1)} %convolution_convert_fusion.3), channel_id=1, replica_groups=mesh['groups'=2,'blk'=4,'tile'=2,'pair'=2] {'blk'}, dimensions={0}, use_global_device_ids=true | all-gather | bytes 983040 | tf_op jit(solution)/shard_map/all_gather | solution.py:130
  111.9 16.3 %all_gather.25 = bf16[1536,256]{1,0:T(8,128)(2,1)} all-gather(bf16[384,256]{1,0:T(8,128)(2,1)S(1)} %convolution_convert_fusion.5), channel_id=1, replica_groups=mesh['groups'=2,'blk'=4,'tile'=2,'pair'=2] {'blk'}, dimensions={0}, use_global_device_ids=true | all-gather | bytes 983040 | tf_op jit(solution)/shard_map/all_gather | solution.py:129
  128.2 1.2 copy.28
  130.2 8.4 %all_gather.26 = bf16[384,768]{1,0:T(8,128)(2,1)S(1)} all-gather(bf16[384,384]{1,0:T(8,128)(2,1)S(1)} %fusion.51), channel_id=1, replica_groups=mesh['groups'=2,'blk'=4,'tile'=2,'pair'=2] {'tile'}, dimensions={1}, use_global_device_ids=true | all-gather | bytes 884736 | tf_op jit(solution)/shard_map/all_gather | solution.py:125
  139.1 1.4 convolution_convert_fusion.4
  140.4 0.8 copy.23
  141.3 19.8 %while.31 = (s32[]{:T(128)}, f32[4,384]{1,0:T(4,128)S(1)}, f32[4,384]{1,0:T(4,128)S(1)}, f32[384,256]{0,1:T(8,128)S(1)}, bf16[2,768,256]{2,1,0:T(8,128)(2,1)}, /...) while((s32[]{:T(128)}, f32[4,384]{1,0:T(4,128)S(1)}, ...), condition=%wide.region_14.15_spmd.clone, body=%wide.region_11.14_spmd.clone.sunk | while | flops 311632896 | bytes 38043784 | solution.py:87
  141.3 1.1 constant_dynamic-slice_fusion.7
  142.6 3.9 %bitcast_reduce_fusion.5 = (f32[4,384]{1,0:T(4,128)S(1)}, f32[4,768,384]{2,1,0:T(8,128)}) fusion(bf16[768,4,64]{0,2,1:T(8,128)(2,1)S(1)} %bitcast.188, bf16[384,4,64]{0,2,1:T(8,128)(2,1)} %bitcast.198), kind=kOutput, calls=%fused_computation.19.clone.1 | convolution fusion | flops 153352704 | bytes 5314560 | tf_op jit(solution)/shard_map/while/body/eval_jaxpr/qhd,khd->hqk/dot_general | solution.py:54
  146.6 3.5 %fusion.120 = f32[384,4,64]{0,2,1:T(8,128)S(1)} fusion(bf16[768,4,64]{0,2,1:T(8,128)(2,1)S(1)} %bitcast.189, f32[4,768,384]{2,1,0:T(8,128)} %get-tuple-element.314, f32[4,384]{1,0:T(4,128)S(1)} %get-tuple-element.363, f32[384,4,64]{0,2,1:T(8,128)S(1)} %bitcast.190, f32[384,4]{0,1:T(4,128)S(1)} %get-tuple-element.316), kind=kOutput, calls=%fused_computation.27.clone.1 | convolution fusion | flops 154730496 | bytes 5910528 | tf_op jit(solution)/shard_map/while/body/eval_jaxpr/hqk,khd->qhd/dot_general | solution.py:64
  150.4 0.8 fusion.118
  151.2 1.1 constant_dynamic-slice_fusion.7
  152.4 3.9 %bitcast_reduce_fusion.5 = (f32[4,384]{1,0:T(4,128)S(1)}, f32[4,768,384]{2,1,0:T(8,128)}) fusion(bf16[768,4,64]{0,2,1:T(8,128)(2,1)S(1)} %bitcast.188, bf16[384,4,64]{0,2,1:T(8,128)(2,1)} %bitcast.198), kind=kOutput, calls=%fused_computation.19.clone.1 | convolution fusion | flops 153352704 | bytes 5314560 | tf_op jit(solution)/shard_map/while/body/eval_jaxpr/qhd,khd->hqk/dot_general | solution.py:54
  156.5 3.5 %fusion.120 = f32[384,4,64]{0,2,1:T(8,128)S(1)} fusion(bf16[768,4,64]{0,2,1:T(8,128)(2,1)S(1)} %bitcast.189, f32[4,768,384]{2,1,0:T(8,128)} %get-tuple-element.314, f32[4,384]{1,0:T(4,128)S(1)} %get-tuple-element.363, f32[384,4,64]{0,2,1:T(8,128)S(1)} %bitcast.190, f32[384,4]{0,1:T(4,128)S(1)} %get-tuple-element.316), kind=kOutput, calls=%fused_computation.27.clone.1 | convolution fusion | flops 154730496 | bytes 5910528 | tf_op jit(solution)/shard_map/while/body/eval_jaxpr/hqk,khd->qhd/dot_general | solution.py:64
  160.3 0.8 fusion.118
  161.1 1.4 convolution_convert_fusion
  162.5 1.0 copy.29
  163.7 14.7 %reduce-scatter.12.cloned.1.call-done = bf16[384,384]{1,0:T(8,128)(2,1)} async-done(((bf16[768,384]{1,0:T(8,128)(2,1)}), bf16[384,384]{1,0:T(8,128)(2,1)}) %reduce-scatter.12.cloned.1.call-update) | async-done | bytes 294928
  178.4 1.2 copy.30
  179.6 0.9 convolution_convert_fusion.2
  180.5 11.2 %reduce-scatter.8.cloned.1.call-done = bf16[3,64,256]{2,1,0:T(8,128)(2,1)} async-done(((bf16[3,128,256]{2,1,0:T(8,128)(2,1)}), bf16[3,64,256]{2,1,0:T(8,128)(2,1)}) %reduce-scatter.8.cloned.1.call-update) | async-done | bytes 98320 | tf_op jit(solution)/shard_map/reduce_scatter | solution.py:145
  191.7 1.0 broadcast_maximum_fusion
  192.7 3.4 %collective-permute-start = (bf16[1,64,256]{2,1,0:T(8,128)(2,1)S(1)}, bf16[1,64,256]{2,1,0:T(8,128)(2,1)S(1)}, u32[]{:S(2)}, u32[]{:S(2)}) collective-permute-start(bf16[1,64,256]{2,1,0:T(8,128)(2,1)S(1)} %get-tuple-element.205), channel_id=1, source_target_pairs={{0,4},{4,8},{8,12},{1,5},{5,9},{9,13},{2,6},{6,10},{10,14},{3,7},{... | collective-permute-start | bytes 98312 | tf_op jit(solution)/shard_map/ppermute | solution.py:19
  196.1 1.3 collective-permute-start.1
  197.7 4.2 %collective-permute-done.1 = bf16[1,64,256]{2,1,0:T(8,128)(2,1)S(1)} collective-permute-done((bf16[1,64,256]{2,1,0:T(8,128)(2,1)S(1)}, bf16[1,64,256]{2,1,0:T(8,128)(2,1)S(1)}, u32[]{:S(2)}, u32[]{:S(2)}) %collective-permute-start.1) | collective-permute-done | bytes 32800 | tf_op jit(solution)/shard_map/ppermute | solution.py:21
  201.9 2.5 %collective-permute-start.2 = (bf16[5,1,256]{2,1,0:T(2,128)(2,1)S(1)}, bf16[5,1,256]{2,1,0:T(2,128)(2,1)S(1)}, u32[]{:S(2)}, u32[]{:S(2)}) collective-permute-start(bf16[5,1,256]{2,1,0:T(2,128)(2,1)S(1)} %get-tuple-element.204), channel_id=1, source_target_pairs={{0,2},{1,3},{4,6},{5,7},{8,10},{9,11},{12,14},{13,15},{16,18},{17,... | collective-permute-start | bytes 7688 | tf_op jit(solution)/shard_map/ppermute | solution.py:19
  204.4 1.3 collective-permute-start.3
  205.7 4.2 %collective-permute-done.3 = bf16[5,1,256]{2,1,0:T(2,128)(2,1)S(1)} collective-permute-done((bf16[5,1,256]{2,1,0:T(2,128)(2,1)S(1)}, bf16[5,1,256]{2,1,0:T(2,128)(2,1)S(1)}, u32[]{:S(2)}, u32[]{:S(2)}) %collective-permute-start.3) | collective-permute-done | bytes 2592 | tf_op jit(solution)/shard_map/ppermute | solution.py:21
  210.2 1.1 fusion.47
  (88 shorter events, 6.3 us)
Async XLA Ops:
  6.5 203.7 %copy-start = (bf16[3,3,256,256]{3,2,1,0:T(8,128)(2,1)S(1)}, bf16[3,3,256,256]{3,2,1,0:T(8,128)(2,1)}, u32[]{:S(2)}) copy-start(bf16[3,3,256,256]{3,2,1,0:T(8,128)(2,1)} %param.19) | copy-start | bytes 3538948
  6.5 121.6 %reduce-scatter.10.cloned.1.call-start = ((), (), s32[]{:S(2)}) async-start(), calls=%async_computation.4 | async-start | bytes 884736
  17.7 1.8 copy-start.9
  64.6 3.8 %copy-start.1 = (f32[4,768,384]{2,1,0:T(8,128)S(1)}, f32[4,768,384]{2,1,0:T(8,128)}, u32[]{:S(2)}) copy-start(f32[4,768,384]{2,1,0:T(8,128)} %get-tuple-element.301) | copy-start | bytes 14155780 | tf_op jit(solution)/shard_map/while
  74.5 3.8 %copy-start.1 = (f32[4,768,384]{2,1,0:T(8,128)S(1)}, f32[4,768,384]{2,1,0:T(8,128)}, u32[]{:S(2)}) copy-start(f32[4,768,384]{2,1,0:T(8,128)} %get-tuple-element.301) | copy-start | bytes 14155780 | tf_op jit(solution)/shard_map/while
  80.5 1.1 copy-start.7
  81.6 96.8 %reduce-scatter.12.cloned.1.call-start = ((), (), s32[]{:S(2)}) async-start(), calls=%async_computation.5 | async-start | bytes 884736
  94.6 34.8 %copy-start.5 = (bf16[1,384,384]{2,1,0:T(8,128)(2,1)S(1)}, bf16[1,384,384]{2,1,0:T(8,128)(2,1)}, u32[]{:S(2)}) copy-start(bf16[1,384,384]{2,1,0:T(8,128)(2,1)} %param.12) | copy-start | bytes 884740
  129.5 0.7 copy-start.3
  146.6 3.8 %copy-start.2 = (f32[4,768,384]{2,1,0:T(8,128)S(1)}, f32[4,768,384]{2,1,0:T(8,128)}, u32[]{:S(2)}) copy-start(f32[4,768,384]{2,1,0:T(8,128)} %get-tuple-element.314) | copy-start | bytes 14155780 | tf_op jit(solution)/shard_map/while
  156.5 3.8 %copy-start.2 = (f32[4,768,384]{2,1,0:T(8,128)S(1)}, f32[4,768,384]{2,1,0:T(8,128)}, u32[]{:S(2)}) copy-start(f32[4,768,384]{2,1,0:T(8,128)} %get-tuple-element.314) | copy-start | bytes 14155780 | tf_op jit(solution)/shard_map/while
  162.5 17.0 %copy-start.4 = (bf16[384,384]{1,0:T(8,128)(2,1)S(1)}, bf16[384,384]{1,0:T(8,128)(2,1)}, u32[]{:S(2)}) copy-start(bf16[384,384]{1,0:T(8,128)(2,1)} %copy-done.3) | copy-start | bytes 884740
  162.5 17.0 %copy-start.8 = (bf16[384,256]{1,0:T(8,128)(2,1)S(1)}, bf16[384,256]{1,0:T(8,128)(2,1)}, u32[]{:S(2)}) copy-start(bf16[384,256]{1,0:T(8,128)(2,1)} %param.18) | copy-start | bytes 589828
  163.6 28.1 %reduce-scatter.8.cloned.1.call-start = ((), (), s32[]{:S(2)}) async-start(), calls=%async_computation.3 | async-start | bytes 294912 | tf_op jit(solution)/shard_map/reduce_scatter | solution.py:145
  191.7 18.3 %copy-start.6 = (bf16[3,64,256]{2,1,0:T(8,128)(2,1)S(1)}, bf16[3,64,256]{2,1,0:T(8,128)(2,1)}, u32[]{:S(2)}) copy-start(bf16[3,64,256]{2,1,0:T(8,128)(2,1)} %reduce-scatter.8.cloned.1.call-done) | copy-start | bytes 294916
  192.7 5.0 %collective-permute-start = (bf16[1,64,256]{2,1,0:T(8,128)(2,1)S(1)}, bf16[1,64,256]{2,1,0:T(8,128)(2,1)S(1)}, u32[]{:S(2)}, u32[]{:S(2)}) collective-permute-start(bf16[1,64,256]{2,1,0:T(8,128)(2,1)S(1)} %get-tuple-element.205), channel_id=1, source_target_pairs={{0,4},{4,8},{8,12},{1,5},{5,9},{9,13},{2,6},{6,10},{10,14},{3,7},{... | collective-permute-start | bytes 98312 | tf_op jit(solution)/shard_map/ppermute | solution.py:19
  196.1 5.8 %collective-permute-start.1 = (bf16[1,64,256]{2,1,0:T(8,128)(2,1)S(1)}, bf16[1,64,256]{2,1,0:T(8,128)(2,1)S(1)}, u32[]{:S(2)}, u32[]{:S(2)}) collective-permute-start(bf16[1,64,256]{2,1,0:T(8,128)(2,1)S(1)} %get-tuple-element.206), channel_id=1, source_target_pairs={{4,0},{8,4},{12,8},{5,1},{9,5},{13,9},{6,2},{10,6},{14,10},{7,3},{... | collective-permute-start | bytes 98312 | tf_op jit(solution)/shard_map/ppermute | solution.py:21
  201.9 3.8 %collective-permute-start.2 = (bf16[5,1,256]{2,1,0:T(2,128)(2,1)S(1)}, bf16[5,1,256]{2,1,0:T(2,128)(2,1)S(1)}, u32[]{:S(2)}, u32[]{:S(2)}) collective-permute-start(bf16[5,1,256]{2,1,0:T(2,128)(2,1)S(1)} %get-tuple-element.204), channel_id=1, source_target_pairs={{0,2},{1,3},{4,6},{5,7},{8,10},{9,11},{12,14},{13,15},{16,18},{17,... | collective-permute-start | bytes 7688 | tf_op jit(solution)/shard_map/ppermute | solution.py:19
  204.4 5.5 %collective-permute-start.3 = (bf16[5,1,256]{2,1,0:T(2,128)(2,1)S(1)}, bf16[5,1,256]{2,1,0:T(2,128)(2,1)S(1)}, u32[]{:S(2)}, u32[]{:S(2)}) collective-permute-start(bf16[5,1,256]{2,1,0:T(2,128)(2,1)S(1)} %get-tuple-element.203), channel_id=1, source_target_pairs={{2,0},{3,1},{6,4},{7,5},{10,8},{11,9},{14,12},{15,13},{18,16},{19,... | collective-permute-start | bytes 7688 | tf_op jit(solution)/shard_map/ppermute | solution.py:21
Sparse Core Ops, SparseCore 0:
  81.7 14.7 reduce-scatter.9
  163.7 14.6 reduce-scatter.11
  180.7 11.0 reduce-scatter.7
where the time goes:
time: 219 us; the launch traced here: 218 us
  blocking collectives  101 us (46%)
  matrix products  40.5 us (18%)
  waiting for transfers between devices  34.7 us (16%)
  local copies, waits for them, and re-layouts  13.6 us (6%)
  between operations  13.5 us (6%)
  starting transfers between devices  8.52 us (4%)
  other arithmetic  5.96 us (3%)
    all_gather x1, blocking collectives, body(): lax.all_gather(self_key, 'blk', axis=0, tiled=True)  20 us
    all_gather x1, blocking collectives, body(): lax.all_gather(self_value, 'blk', axis=0, tiled=True)  18.1 us
    all_gather x1, blocking collectives, body(): lax.all_gather(cross_value, 'blk', axis=0, tiled=True)  17.3 us
    all_gather x1, blocking collectives, body(): lax.all_gather(cross_key, 'blk', axis=0, tiled=True)  16.3 us
    dot_general x4, matrix products, attend_keys(): jnp.einsum('qhd,khd->hqk', queries.reshape(query_count, head_count, HD),...  15.5 us
    unnamed x5, waiting for transfers between devices  14.8 us
    dot_general x4, matrix products, attend_keys(): jnp.einsum('hqk,khd->qhd', expanded.astype(jnp.bfloat16), values_rows.res...  14 us
    reduce_scatter x1, waiting for transfers between devices, body(): lax.psum_scatter(partial_map.astype(jnp.bfloat16), 'tile', scatter_dimens...  11.2 us
  transfers between devices with their start and end apart: 7, of which 5 were waited for; matrix products, arithmetic and copies ran while one was open for 1% of the time, Pallas kernels for 0%

commit v1 on v0

--- a/solution.py
+++ b/solution.py
@@ -99,6 +99,25 @@
 def body(
     left_tokens, right_tokens, self_qkv, self_out, cross_qkv, cross_out, reassemble, conv_weight
 ):
+
+    def _lead_rails(x_local):
+        num_devices = lax.psum(1, "blk")
+        nodes = []
+        for to_i in range(num_devices):
+            nodes.append((to_i, (to_i + 1) % num_devices))
+        copies = []
+        for to_i in range(num_devices):
+            copies.append((to_i, (to_i - 1) % num_devices))
+        b_next, back = ([x_local], [x_local])
+        for _ in range(num_devices // 2):
+            b_next.append(lax.ppermute(b_next[-1], "blk", perm=nodes))
+        for _ in range((num_devices - 1) // 2):
+            back.append(lax.ppermute(back[-1], perm=copies, axis_name="blk"))
+        everything = jnp.concatenate([*b_next[::-1], *back[1:]], 0)
+        return jnp.roll(
+            everything, (lax.axis_index("blk") - num_devices // 2) * x_local.shape[0], 0
+        )
+
     left_full, right_full = (
         lax.all_gather(left_tokens, "tile", axis=2, tiled=True),
         lax.all_gather(right_tokens, "tile", axis=2, tiled=True),
@@ -111,10 +130,7 @@
     self_value = project_rows(left_normed, self_qkv[2])
     cross_key = project_rows(right_normed, cross_qkv[1])
     cross_value = project_rows(right_normed, cross_qkv[2])
-    pieces = (
-        lax.all_gather(self_key, "blk", axis=0, tiled=True),
-        lax.all_gather(self_value, "blk", axis=0, tiled=True),
-    )
+    pieces = (lax.all_gather(self_key, "blk", axis=0, tiled=True), _lead_rails(self_value))
     self_state = fold_keys(initial_state(self_query), self_query, pieces[0], pieces[1])
     self_mixed = finish_state(self_state)
     self_term = jnp.dot(self_mixed, self_out, preferred_element_type=jnp.float32)

time: 219 us -> 212 us (0.968)
  blocking collectives: 101 us -> 81.9 us
  waiting for transfers between devices: 34.7 us -> 40.7 us
  starting transfers between devices: 8.52 us -> 13.4 us
    all_gather x1 -> x0, blocking collectives: 18.1 us -> none  [body(): lax.all_gather(self_value, 'blk', axis=0, tiled=True)]
    ppermute x0 -> x3, starting transfers between devices: none -> 4.93 us  [the longest x2 2.83 us: _lead_rails(): b_next.append(lax.ppermute(b_next[-1], 'blk', perm=nodes))]
    ppermute x0 -> x3, waiting for transfers between devices: none -> 4.81 us  [the longest x2 4.81 us: _lead_rails(): b_next.append(lax.ppermute(b_next[-1], 'blk', perm=nodes))]
    all_gather x1, blocking collectives: 9.72 us -> 7.38 us  [body(): lax.all_gather(right_tokens, 'tile', axis=2, tiled=True)]
    unnamed x27 -> x44, local copies, waits for them, and re-layouts: 6.94 us -> 7.05 us
  transfers between devices with their start and end apart: 7 -> 10, of which waited for: 5 -> 6; matrix products, arithmetic and copies ran while one was open for 1% -> 3% of each run, Pallas kernels for 0% -> 0%
where the time goes in v1:
time: 212 us; the launch traced here: 211 us
  blocking collectives  81.9 us (39%)
  waiting for transfers between devices  40.7 us (19%)
  matrix products  40.5 us (19%)
  local copies, waits for them, and re-layouts  14 us (7%)
  between operations  13.6 us (6%)
  starting transfers between devices  13.4 us (6%)
  other arithmetic  6.53 us (3%)
    all_gather x1, blocking collectives, body(): lax.all_gather(self_key, 'blk', axis=0, tiled=True)  21.9 us
    all_gather x1, blocking collectives, body(): lax.all_gather(cross_value, 'blk', axis=0, tiled=True)  17.7 us
    all_gather x1, blocking collectives, body(): lax.all_gather(cross_key, 'blk', axis=0, tiled=True)  16.3 us
    unnamed x5, waiting for transfers between devices  16 us
    dot_general x4, matrix products, attend_keys(): jnp.einsum('qhd,khd->hqk', queries.reshape(query_count, head_count, HD),...  15.5 us
    dot_general x4, matrix products, attend_keys(): jnp.einsum('hqk,khd->qhd', expanded.astype(jnp.bfloat16), values_rows.res...  14 us
    reduce_scatter x1, waiting for transfers between devices, body(): lax.psum_scatter(partial_map.astype(jnp.bfloat16), 'tile', scatter_dimens...  11.2 us
    all_gather x1, blocking collectives, body(): lax.all_gather(left_tokens, 'tile', axis=2, tiled=True)  11 us
  transfers between devices with their start and end apart: 10, of which 6 were waited for; matrix products, arithmetic and copies ran while one was open for 3% of the time, Pallas kernels for 0%

profile of v1, /device:TPU:0, one launch (start us, length us, event | category | flops | bytes accessed | tf_op | source)
XLA Modules:
  0.0 210.8 jit_solution(2752539351493203461)
XLA Ops:
  6.5 11.0 %all_gather.18 = bf16[1,384,768]{2,1,0:T(8,128)(2,1)S(1)} all-gather(bf16[1,384,384]{2,1,0:T(8,128)(2,1)} %param.12), channel_id=1, replica_groups=mesh['groups'=2,'blk'=4,'tile'=2,'pair'=2] {'tile'}, dimensions={2}, use_global_device_ids=true | all-gather | bytes 884736 | tf_op jit(solution)/shard_map/all_gather | solution.py:122
  18.1 1.4 convolution_convert_fusion.6
  19.5 1.8 collective-permute-start
  21.3 2.1 collective-permute-start.2
  24.2 21.9 %all_gather.19 = bf16[1536,256]{1,0:T(8,128)(2,1)} all-gather(bf16[384,256]{1,0:T(8,128)(2,1)S(1)} %convolution_convert_fusion.8), channel_id=1, replica_groups=mesh['groups'=2,'blk'=4,'tile'=2,'pair'=2] {'blk'}, dimensions={0}, use_global_device_ids=true | all-gather | bytes 983040 | tf_op jit(solution)/shard_map/all_gather | solution.py:133
  46.1 7.4 %all_gather.20 = bf16[1,384,768]{2,1,0:T(8,128)(2,1)S(1)} all-gather(bf16[1,384,384]{2,1,0:T(8,128)(2,1)S(1)} %copy-done.9), channel_id=1, replica_groups=mesh['groups'=2,'blk'=4,'tile'=2,'pair'=2] {'tile'}, dimensions={2}, use_global_device_ids=true | all-gather | bytes 884736 | tf_op jit(solution)/shard_map/all_gather | solution.py:123
  53.6 1.0 collective-permute-start.1
  54.7 0.8 copy.27
  55.5 0.9 fusion.45
  56.3 4.8 %collective-permute-done.1 = bf16[384,256]{1,0:T(8,128)(2,1)S(1)} collective-permute-done((bf16[384,256]{1,0:T(8,128)(2,1)S(1)}, bf16[384,256]{1,0:T(8,128)(2,1)S(1)}, u32[]{:S(2)}, u32[]{:S(2)}) %collective-permute-start.1) | collective-permute-done | bytes 196640 | tf_op jit(solution)/shard_map/ppermute | solution.py:113
  61.6 19.8 %while.30 = (s32[]{:T(128)}, f32[4,384]{1,0:T(4,128)S(1)}, f32[4,384]{1,0:T(4,128)S(1)}, f32[384,256]{0,1:T(8,128)S(1)}, bf16[2,768,256]{2,1,0:T(8,128)(2,1)}, /...) while((s32[]{:T(128)}, f32[4,384]{1,0:T(4,128)S(1)}, ...), condition=%wide.region_5.6_spmd.clone, body=%wide.region_2.5_spmd.clone.sunk | while | flops 311632896 | bytes 38043784 | solution.py:87
  61.6 1.1 constant_dynamic-slice_fusion.7
  62.9 3.9 %bitcast_reduce_fusion.4 = (f32[4,384]{1,0:T(4,128)S(1)}, f32[4,768,384]{2,1,0:T(8,128)}) fusion(bf16[768,4,64]{0,2,1:T(8,128)(2,1)S(1)} %bitcast.186, bf16[384,4,64]{0,2,1:T(8,128)(2,1)} %bitcast.198), kind=kOutput, calls=%fused_computation.1.clone.1 | convolution fusion | flops 153352704 | bytes 5314560 | tf_op jit(solution)/shard_map/while/body/eval_jaxpr/qhd,khd->hqk/dot_general | solution.py:54
  66.9 3.5 %fusion.112 = f32[384,4,64]{0,2,1:T(8,128)S(1)} fusion(bf16[768,4,64]{0,2,1:T(8,128)(2,1)S(1)} %bitcast.187, f32[4,768,384]{2,1,0:T(8,128)} %get-tuple-element.315, f32[4,384]{1,0:T(4,128)S(1)} %get-tuple-element.350, f32[384,4,64]{0,2,1:T(8,128)S(1)} %bitcast.192, f32[384,4]{0,1:T(4,128)S(1)} %get-tuple-element.317), kind=kOutput, calls=%fused_computation.9.clone.1 | convolution fusion | flops 154730496 | bytes 5910528 | tf_op jit(solution)/shard_map/while/body/eval_jaxpr/hqk,khd->qhd/dot_general | solution.py:64
  71.5 1.1 constant_dynamic-slice_fusion.7
  72.7 3.9 %bitcast_reduce_fusion.4 = (f32[4,384]{1,0:T(4,128)S(1)}, f32[4,768,384]{2,1,0:T(8,128)}) fusion(bf16[768,4,64]{0,2,1:T(8,128)(2,1)S(1)} %bitcast.186, bf16[384,4,64]{0,2,1:T(8,128)(2,1)} %bitcast.198), kind=kOutput, calls=%fused_computation.1.clone.1 | convolution fusion | flops 153352704 | bytes 5314560 | tf_op jit(solution)/shard_map/while/body/eval_jaxpr/qhd,khd->hqk/dot_general | solution.py:54
  76.8 3.5 %fusion.112 = f32[384,4,64]{0,2,1:T(8,128)S(1)} fusion(bf16[768,4,64]{0,2,1:T(8,128)(2,1)S(1)} %bitcast.187, f32[4,768,384]{2,1,0:T(8,128)} %get-tuple-element.315, f32[4,384]{1,0:T(4,128)S(1)} %get-tuple-element.350, f32[384,4,64]{0,2,1:T(8,128)S(1)} %bitcast.192, f32[384,4]{0,1:T(4,128)S(1)} %get-tuple-element.317), kind=kOutput, calls=%fused_computation.9.clone.1 | convolution fusion | flops 154730496 | bytes 5910528 | tf_op jit(solution)/shard_map/while/body/eval_jaxpr/hqk,khd->qhd/dot_general | solution.py:64
  81.4 1.4 convolution_convert_fusion.1
  82.8 1.1 copy.34
  84.0 1.4 convolution_convert_fusion.3
  85.4 1.4 convolution_convert_fusion.5
  86.8 17.7 %all_gather.23 = bf16[1536,256]{1,0:T(8,128)(2,1)S(1)} all-gather(bf16[384,256]{1,0:T(8,128)(2,1)S(1)} %convolution_convert_fusion.3), channel_id=1, replica_groups=mesh['groups'=2,'blk'=4,'tile'=2,'pair'=2] {'blk'}, dimensions={0}, use_global_device_ids=true | all-gather | bytes 983040 | tf_op jit(solution)/shard_map/all_gather | solution.py:146
  104.5 16.3 %all_gather.21 = bf16[1536,256]{1,0:T(8,128)(2,1)} all-gather(bf16[384,256]{1,0:T(8,128)(2,1)S(1)} %convolution_convert_fusion.5), channel_id=1, replica_groups=mesh['groups'=2,'blk'=4,'tile'=2,'pair'=2] {'blk'}, dimensions={0}, use_global_device_ids=true | all-gather | bytes 983040 | tf_op jit(solution)/shard_map/all_gather | solution.py:145
  120.8 1.2 copy.35
  122.8 7.6 %all_gather.22 = bf16[384,768]{1,0:T(8,128)(2,1)S(1)} all-gather(bf16[384,384]{1,0:T(8,128)(2,1)S(1)} %fusion.51), channel_id=1, replica_groups=mesh['groups'=2,'blk'=4,'tile'=2,'pair'=2] {'tile'}, dimensions={1}, use_global_device_ids=true | all-gather | bytes 884736 | tf_op jit(solution)/shard_map/all_gather | solution.py:141
  130.9 1.4 convolution_convert_fusion.4
  132.2 0.8 copy.30
  133.1 19.8 %while.31 = (s32[]{:T(128)}, f32[4,384]{1,0:T(4,128)S(1)}, f32[4,384]{1,0:T(4,128)S(1)}, f32[384,256]{0,1:T(8,128)S(1)}, bf16[2,768,256]{2,1,0:T(8,128)(2,1)}, /...) while((s32[]{:T(128)}, f32[4,384]{1,0:T(4,128)S(1)}, ...), condition=%wide.region_14.15_spmd.clone, body=%wide.region_11.14_spmd.clone.sunk | while | flops 311632896 | bytes 38043784 | solution.py:87
  133.1 1.1 constant_dynamic-slice_fusion.8
  134.3 3.9 %bitcast_reduce_fusion.5 = (f32[4,384]{1,0:T(4,128)S(1)}, f32[4,768,384]{2,1,0:T(8,128)}) fusion(bf16[768,4,64]{0,2,1:T(8,128)(2,1)S(1)} %bitcast.188, bf16[384,4,64]{0,2,1:T(8,128)(2,1)} %bitcast.199), kind=kOutput, calls=%fused_computation.19.clone.1 | convolution fusion | flops 153352704 | bytes 5314560 | tf_op jit(solution)/shard_map/while/body/eval_jaxpr/qhd,khd->hqk/dot_general | solution.py:54
  138.4 3.5 %fusion.120 = f32[384,4,64]{0,2,1:T(8,128)S(1)} fusion(bf16[768,4,64]{0,2,1:T(8,128)(2,1)S(1)} %bitcast.189, f32[4,768,384]{2,1,0:T(8,128)} %get-tuple-element.328, f32[4,384]{1,0:T(4,128)S(1)} %get-tuple-element.377, f32[384,4,64]{0,2,1:T(8,128)S(1)} %bitcast.190, f32[384,4]{0,1:T(4,128)S(1)} %get-tuple-element.330), kind=kOutput, calls=%fused_computation.27.clone.1 | convolution fusion | flops 154730496 | bytes 5910528 | tf_op jit(solution)/shard_map/while/body/eval_jaxpr/hqk,khd->qhd/dot_general | solution.py:64
  143.0 1.1 constant_dynamic-slice_fusion.8
  144.2 3.9 %bitcast_reduce_fusion.5 = (f32[4,384]{1,0:T(4,128)S(1)}, f32[4,768,384]{2,1,0:T(8,128)}) fusion(bf16[768,4,64]{0,2,1:T(8,128)(2,1)S(1)} %bitcast.188, bf16[384,4,64]{0,2,1:T(8,128)(2,1)} %bitcast.199), kind=kOutput, calls=%fused_computation.19.clone.1 | convolution fusion | flops 153352704 | bytes 5314560 | tf_op jit(solution)/shard_map/while/body/eval_jaxpr/qhd,khd->hqk/dot_general | solution.py:54
  148.3 3.5 %fusion.120 = f32[384,4,64]{0,2,1:T(8,128)S(1)} fusion(bf16[768,4,64]{0,2,1:T(8,128)(2,1)S(1)} %bitcast.189, f32[4,768,384]{2,1,0:T(8,128)} %get-tuple-element.328, f32[4,384]{1,0:T(4,128)S(1)} %get-tuple-element.377, f32[384,4,64]{0,2,1:T(8,128)S(1)} %bitcast.190, f32[384,4]{0,1:T(4,128)S(1)} %get-tuple-element.330), kind=kOutput, calls=%fused_computation.27.clone.1 | convolution fusion | flops 154730496 | bytes 5910528 | tf_op jit(solution)/shard_map/while/body/eval_jaxpr/hqk,khd->qhd/dot_general | solution.py:64
  152.9 1.4 convolution_convert_fusion
  154.3 1.1 copy.36
  155.5 16.0 %reduce-scatter.12.cloned.1.call-done = bf16[384,384]{1,0:T(8,128)(2,1)} async-done(((bf16[768,384]{1,0:T(8,128)(2,1)}), bf16[384,384]{1,0:T(8,128)(2,1)}) %reduce-scatter.12.cloned.1.call-update) | async-done | bytes 294928
  171.4 1.2 copy.37
  172.6 0.9 convolution_convert_fusion.2
  173.6 11.2 %reduce-scatter.8.cloned.1.call-done = bf16[3,64,256]{2,1,0:T(8,128)(2,1)} async-done(((bf16[3,128,256]{2,1,0:T(8,128)(2,1)}), bf16[3,64,256]{2,1,0:T(8,128)(2,1)}) %reduce-scatter.8.cloned.1.call-update) | async-done | bytes 98320 | tf_op jit(solution)/shard_map/reduce_scatter | solution.py:161
  184.8 1.0 broadcast_maximum_fusion
  185.8 3.4 %collective-permute-start.3 = (bf16[1,64,256]{2,1,0:T(8,128)(2,1)S(1)}, bf16[1,64,256]{2,1,0:T(8,128)(2,1)S(1)}, u32[]{:S(2)}, u32[]{:S(2)}) collective-permute-start(bf16[1,64,256]{2,1,0:T(8,128)(2,1)S(1)} %get-tuple-element.219), channel_id=1, source_target_pairs={{0,4},{4,8},{8,12},{1,5},{5,9},{9,13},{2,6},{6,10},{10,14},{3,7},{... | collective-permute-start | bytes 98312 | tf_op jit(solution)/shard_map/ppermute | solution.py:19
  189.1 1.3 collective-permute-start.4
  190.7 4.2 %collective-permute-done.4 = bf16[1,64,256]{2,1,0:T(8,128)(2,1)S(1)} collective-permute-done((bf16[1,64,256]{2,1,0:T(8,128)(2,1)S(1)}, bf16[1,64,256]{2,1,0:T(8,128)(2,1)S(1)}, u32[]{:S(2)}, u32[]{:S(2)}) %collective-permute-start.4) | collective-permute-done | bytes 32800 | tf_op jit(solution)/shard_map/ppermute | solution.py:21
  195.0 2.5 %collective-permute-start.5 = (bf16[5,1,256]{2,1,0:T(2,128)(2,1)S(1)}, bf16[5,1,256]{2,1,0:T(2,128)(2,1)S(1)}, u32[]{:S(2)}, u32[]{:S(2)}) collective-permute-start(bf16[5,1,256]{2,1,0:T(2,128)(2,1)S(1)} %get-tuple-element.218), channel_id=1, source_target_pairs={{0,2},{1,3},{4,6},{5,7},{8,10},{9,11},{12,14},{13,15},{16,18},{17,... | collective-permute-start | bytes 7688 | tf_op jit(solution)/shard_map/ppermute | solution.py:19
  197.4 1.3 collective-permute-start.6
  198.8 4.2 %collective-permute-done.6 = bf16[5,1,256]{2,1,0:T(2,128)(2,1)S(1)} collective-permute-done((bf16[5,1,256]{2,1,0:T(2,128)(2,1)S(1)}, bf16[5,1,256]{2,1,0:T(2,128)(2,1)S(1)}, u32[]{:S(2)}, u32[]{:S(2)}) %collective-permute-start.6) | collective-permute-done | bytes 2592 | tf_op jit(solution)/shard_map/ppermute | solution.py:21
  203.3 1.1 fusion.47
  (112 shorter events, 9.5 us)
Async XLA Ops:
  6.5 196.7 %copy-start = (bf16[3,3,256,256]{3,2,1,0:T(8,128)(2,1)S(1)}, bf16[3,3,256,256]{3,2,1,0:T(8,128)(2,1)}, u32[]{:S(2)}) copy-start(bf16[3,3,256,256]{3,2,1,0:T(8,128)(2,1)} %param.19) | copy-start | bytes 3538948
  6.5 114.3 %reduce-scatter.10.cloned.1.call-start = ((), (), s32[]{:S(2)}) async-start(), calls=%async_computation.4 | async-start | bytes 884736
  17.7 5.7 %copy-start.14 = (bf16[3,768,256]{2,1,0:T(8,128)(2,1)S(1)}, bf16[3,768,256]{2,1,0:T(8,128)(2,1)}, u32[]{:S(2)}) copy-start(bf16[3,768,256]{2,1,0:T(8,128)(2,1)} %param.14) | copy-start | bytes 3538948
  19.5 34.2 %collective-permute-start = (bf16[384,256]{1,0:T(8,128)(2,1)S(1)}, bf16[384,256]{1,0:T(8,128)(2,1)S(1)}, u32[]{:S(2)}, u32[]{:S(2)}) collective-permute-start(bf16[384,256]{1,0:T(8,128)(2,1)S(1)} %convolution_convert_fusion.6), channel_id=1, source_target_pairs={{0,4},{4,8},{8,12},{12,0},{1,5},{5,9},{9,13},{13,1},{2,6},{6,10},{... | collective-permute-start | bytes 589832 | tf_op jit(solution)/shard_map/ppermute | solution.py:113
  21.3 39.9 %collective-permute-start.2 = (bf16[384,256]{1,0:T(8,128)(2,1)S(1)}, bf16[384,256]{1,0:T(8,128)(2,1)S(1)}, u32[]{:S(2)}, u32[]{:S(2)}) collective-permute-start(bf16[384,256]{1,0:T(8,128)(2,1)S(1)} %convolution_convert_fusion.6), channel_id=1, source_target_pairs={{0,12},{4,0},{8,4},{12,8},{1,13},{5,1},{9,5},{13,9},{2,14},{6,2},{... | collective-permute-start | bytes 589832 | tf_op jit(solution)/shard_map/ppermute | solution.py:115
  23.8 22.3 %copy-start.9 = (bf16[1,384,384]{2,1,0:T(8,128)(2,1)S(1)}, bf16[1,384,384]{2,1,0:T(8,128)(2,1)}, u32[]{:S(2)}) copy-start(bf16[1,384,384]{2,1,0:T(8,128)(2,1)} %param.13) | copy-start | bytes 884740
  53.5 7.7 %copy-start.3 = (bf16[1,384,768]{2,1,0:T(8,128)(2,1)}, bf16[1,384,768]{2,1,0:T(8,128)(2,1)S(1)}, u32[]{:S(2)}) copy-start(bf16[1,384,768]{2,1,0:T(8,128)(2,1)S(1)} %all_gather.20) | copy-start | bytes 1769476
  53.6 7.5 %collective-permute-start.1 = (bf16[384,256]{1,0:T(8,128)(2,1)S(1)}, bf16[384,256]{1,0:T(8,128)(2,1)S(1)}, u32[]{:S(2)}, u32[]{:S(2)}) collective-permute-start(bf16[384,256]{1,0:T(8,128)(2,1)S(1)} %collective-permute-done), channel_id=1, source_target_pairs={{0,4},{4,8},{8,12},{12,0},{1,5},{5,9},{9,13},{13,1},{2,6},{6,10},{... | collective-permute-start | bytes 589832 | tf_op jit(solution)/shard_map/ppermute | solution.py:113
  54.6 6.6 %copy-start.11 = (f32[384]{0:T(512)}, f32[384]{0:T(512)S(1)}, u32[]{:S(2)}) copy-start(f32[384]{0:T(512)S(1)} %broadcast_multiply_fusion.1) | copy-start | bytes 4612
  66.9 3.8 %copy-start.1 = (f32[4,768,384]{2,1,0:T(8,128)S(1)}, f32[4,768,384]{2,1,0:T(8,128)}, u32[]{:S(2)}) copy-start(f32[4,768,384]{2,1,0:T(8,128)} %get-tuple-element.315) | copy-start | bytes 14155780 | tf_op jit(solution)/shard_map/while
  76.8 3.8 %copy-start.1 = (f32[4,768,384]{2,1,0:T(8,128)S(1)}, f32[4,768,384]{2,1,0:T(8,128)}, u32[]{:S(2)}) copy-start(f32[4,768,384]{2,1,0:T(8,128)} %get-tuple-element.315) | copy-start | bytes 14155780 | tf_op jit(solution)/shard_map/while
  82.8 1.2 copy-start.13
  82.8 1.2 copy-start.4
  82.8 1.2 copy-start.12
  83.9 87.5 %reduce-scatter.12.cloned.1.call-start = ((), (), s32[]{:S(2)}) async-start(), calls=%async_computation.5 | async-start | bytes 884736
  86.8 35.2 %copy-start.7 = (bf16[1,384,384]{2,1,0:T(8,128)(2,1)S(1)}, bf16[1,384,384]{2,1,0:T(8,128)(2,1)}, u32[]{:S(2)}) copy-start(bf16[1,384,384]{2,1,0:T(8,128)(2,1)} %param.12) | copy-start | bytes 884740
  122.1 0.7 copy-start.5
  138.4 3.8 %copy-start.2 = (f32[4,768,384]{2,1,0:T(8,128)S(1)}, f32[4,768,384]{2,1,0:T(8,128)}, u32[]{:S(2)}) copy-start(f32[4,768,384]{2,1,0:T(8,128)} %get-tuple-element.328) | copy-start | bytes 14155780 | tf_op jit(solution)/shard_map/while
  148.3 3.8 %copy-start.2 = (f32[4,768,384]{2,1,0:T(8,128)S(1)}, f32[4,768,384]{2,1,0:T(8,128)}, u32[]{:S(2)}) copy-start(f32[4,768,384]{2,1,0:T(8,128)} %get-tuple-element.328) | copy-start | bytes 14155780 | tf_op jit(solution)/shard_map/while
  154.3 18.3 %copy-start.6 = (bf16[384,384]{1,0:T(8,128)(2,1)S(1)}, bf16[384,384]{1,0:T(8,128)(2,1)}, u32[]{:S(2)}) copy-start(bf16[384,384]{1,0:T(8,128)(2,1)} %copy-done.5) | copy-start | bytes 884740
  154.3 18.3 %copy-start.10 = (bf16[384,256]{1,0:T(8,128)(2,1)S(1)}, bf16[384,256]{1,0:T(8,128)(2,1)}, u32[]{:S(2)}) copy-start(bf16[384,256]{1,0:T(8,128)(2,1)} %param.18) | copy-start | bytes 589828
  155.4 29.4 %reduce-scatter.8.cloned.1.call-start = ((), (), s32[]{:S(2)}) async-start(), calls=%async_computation.3 | async-start | bytes 294912 | tf_op jit(solution)/shard_map/reduce_scatter | solution.py:161
  184.8 18.3 %copy-start.8 = (bf16[3,64,256]{2,1,0:T(8,128)(2,1)S(1)}, bf16[3,64,256]{2,1,0:T(8,128)(2,1)}, u32[]{:S(2)}) copy-start(bf16[3,64,256]{2,1,0:T(8,128)(2,1)} %reduce-scatter.8.cloned.1.call-done) | copy-start | bytes 294916
  185.8 5.0 %collective-permute-start.3 = (bf16[1,64,256]{2,1,0:T(8,128)(2,1)S(1)}, bf16[1,64,256]{2,1,0:T(8,128)(2,1)S(1)}, u32[]{:S(2)}, u32[]{:S(2)}) collective-permute-start(bf16[1,64,256]{2,1,0:T(8,128)(2,1)S(1)} %get-tuple-element.219), channel_id=1, source_target_pairs={{0,4},{4,8},{8,12},{1,5},{5,9},{9,13},{2,6},{6,10},{10,14},{3,7},{... | collective-permute-start | bytes 98312 | tf_op jit(solution)/shard_map/ppermute | solution.py:19
  189.1 5.8 %collective-permute-start.4 = (bf16[1,64,256]{2,1,0:T(8,128)(2,1)S(1)}, bf16[1,64,256]{2,1,0:T(8,128)(2,1)S(1)}, u32[]{:S(2)}, u32[]{:S(2)}) collective-permute-start(bf16[1,64,256]{2,1,0:T(8,128)(2,1)S(1)} %get-tuple-element.220), channel_id=1, source_target_pairs={{4,0},{8,4},{12,8},{5,1},{9,5},{13,9},{6,2},{10,6},{14,10},{7,3},{... | collective-permute-start | bytes 98312 | tf_op jit(solution)/shard_map/ppermute | solution.py:21
  195.0 3.8 %collective-permute-start.5 = (bf16[5,1,256]{2,1,0:T(2,128)(2,1)S(1)}, bf16[5,1,256]{2,1,0:T(2,128)(2,1)S(1)}, u32[]{:S(2)}, u32[]{:S(2)}) collective-permute-start(bf16[5,1,256]{2,1,0:T(2,128)(2,1)S(1)} %get-tuple-element.218), channel_id=1, source_target_pairs={{0,2},{1,3},{4,6},{5,7},{8,10},{9,11},{12,14},{13,15},{16,18},{17,... | collective-permute-start | bytes 7688 | tf_op jit(solution)/shard_map/ppermute | solution.py:19
  197.4 5.5 %collective-permute-start.6 = (bf16[5,1,256]{2,1,0:T(2,128)(2,1)S(1)}, bf16[5,1,256]{2,1,0:T(2,128)(2,1)S(1)}, u32[]{:S(2)}, u32[]{:S(2)}) collective-permute-start(bf16[5,1,256]{2,1,0:T(2,128)(2,1)S(1)} %get-tuple-element.217), channel_id=1, source_target_pairs={{2,0},{3,1},{6,4},{7,5},{10,8},{11,9},{14,12},{15,13},{18,16},{19,... | collective-permute-start | bytes 7688 | tf_op jit(solution)/shard_map/ppermute | solution.py:21
Sparse Core Ops, SparseCore 0:
  84.0 14.1 reduce-scatter.9
  155.5 15.8 reduce-scatter.11
  173.7 11.0 reduce-scatter.7
